TPU v7x, 32 devices: a whole 2x2x4 slice. The times are simulated.
32 devices in a mesh: grp: 2 (over y), rows: 4 (over z), img: 2 (over x), tp: 2 (over core).
Axes of the slice: x: 2, y: 2, z: 4, core: 2. Of those that a mesh axis runs over, the one named last changes fastest.
Arguments:
- features: bfloat16 [16, 28, 2, 7168], P(('grp', 'img'), 'rows', 'tp'), parts along dimension 0, may hold values from -8 to 8
- gn_gain: float32 [128], P('tp'), may hold values from 0.5 to 1.5
- conv_w: bfloat16 [3, 3, 3, 128], P(None, None, None, 'tp'), may hold values from -0.1875 to 0.1875
- patch_w: bfloat16 [1280, 588], P('rows'), may hold values from -0.25 to 0.25
- pos_emb: bfloat16 [64, 1280], replicated, may hold values from -3 to 3
- ln1_gain: float32 [1280], replicated, may hold values from 0.5 to 1.5
- qkv_w: bfloat16 [1280, 3, 1280], P('rows', None, 'tp'), may hold values from -3 to 3
- out_w: bfloat16 [1280, 1280], P('rows', 'tp'), may hold values from -0.15625 to 0.15625
- final_gain: float32 [1280], replicated, may hold values from 0.5 to 1.5
- head_w: float32 [1280], replicated, may hold values from -0.15625 to 0.15625
- owner_slot: int32 [4, 4], P(('grp', 'img')), parts along dimension 0, may hold values from 0 to 3, each once within a row
Outputs:
- grad_features: bfloat16 [16, 28, 2, 7168], P(('grp', 'img'), 'rows', 'tp'), parts along dimension 0
- slot_reward: float32 [16], P(('grp', 'img', 'rows')), parts along dimension 0
There are 2 independent parts, one for each index of `grp`. A program takes and returns all parts, laid end to end along the dimension named above; an argument that names none is the same for every part. Nothing has to cross between parts.
Inputs may be any that keep to these rules, and one draw needn't show every extreme that they name: Each row is a permutation: image g * 4 + j is scored in slot owner_slot[g, j] of its image group.
All inputs are finite; a program needn't handle non-finite values.
Results may differ from a plain program's by a relative error of at most 0.028.
Values may be sent and summed in bfloat16 or wider, within the bound.
A program may use at most 128 MiB of HBM per device.

v0:
```python
import math
import jax
import jax.numpy as jnp
from jax import lax
from jax.sharding import PartitionSpec as P

C = 128
GROUPS = 32
PATCH = 14
HEAD_DIM = 80
W = 112
EPS_GROUP = 1e-06
EPS_LAYER = 1e-05


def padded_2(block, sides, width):
    for axis, dim in sides:
        count = lax.axis_size(axis)
        forward = [(i, i + 1) for i in range(count - 1)]
        backward = [(target, source) for source, target in forward]
        low = lax.ppermute(
            lax.slice_in_dim(block, block.shape[dim] - width, None, axis=dim), axis, forward
        )
        high = lax.ppermute(lax.slice_in_dim(block, 0, width, axis=dim), axis, backward)
        block = jnp.concatenate([low, block, high], axis=dim)
    return block


def round_half(values):
    return lax.optimization_barrier(values.astype(jnp.bfloat16)).astype(jnp.float32)


def layer_norm(values, scale_vec):
    average = jnp.mean(values, axis=-1, keepdims=True)
    centred = values - average
    spread = jnp.mean(centred * centred, axis=-1, keepdims=True)
    inverse = lax.rsqrt(spread + EPS_LAYER)
    normed = centred * inverse
    return (normed * scale_vec, normed, inverse)


def layer_norm_back(upstream, normed, inverse, scale_vec):
    scaled = upstream * scale_vec
    mean_one = jnp.mean(scaled, axis=-1, keepdims=True)
    mean_two = jnp.mean(scaled * normed, axis=-1, keepdims=True)
    return inverse * (scaled - mean_one - normed * mean_two)


def silu_parts(values):
    sigmoid = jax.nn.sigmoid(values)
    return (values * sigmoid, sigmoid * (1.0 + values * (1.0 - sigmoid)))


def soft_weights(q_heads, k_heads):
    factor = 1.0 / math.sqrt(HEAD_DIM)
    scores = jnp.einsum("thd,shd->hts", q_heads, k_heads) * factor
    row_max = jnp.max(scores, axis=-1, keepdims=True)
    exp_scores = jnp.exp(scores - row_max)
    return exp_scores / jnp.sum(exp_scores, axis=-1, keepdims=True)


def split_heads(rows_in):
    return rows_in.reshape(rows_in.shape[0], rows_in.shape[1] // HEAD_DIM, HEAD_DIM).astype(
        jnp.float32
    )


def attend(queries, key_rows, value_rows):
    prob_soft = soft_weights(split_heads(queries), split_heads(key_rows))
    attended = jnp.einsum("hts,shd->thd", round_half(prob_soft), split_heads(value_rows))
    return attended.reshape(queries.shape).astype(jnp.bfloat16)


def attend_back(queries, key_rows, value_rows, head_grad):
    factor = 1.0 / math.sqrt(HEAD_DIM)
    q_heads = split_heads(queries)
    k_heads = split_heads(key_rows)
    v_heads = split_heads(value_rows)
    g_heads = split_heads(head_grad)
    prob_soft = soft_weights(q_heads, k_heads)
    dprob = jnp.einsum("thd,shd->hts", g_heads, v_heads)
    dvalue = (
        jnp.einsum("hts,thd->shd", round_half(prob_soft), g_heads)
        .reshape(queries.shape)
        .astype(jnp.bfloat16)
    )
    dscores = prob_soft * (dprob - jnp.sum(dprob * prob_soft, axis=-1, keepdims=True)) * factor
    dscores = round_half(dscores)
    dquery = (
        jnp.einsum("hts,shd->thd", dscores, k_heads).reshape(queries.shape).astype(jnp.bfloat16)
    )
    dkey = jnp.einsum("hts,thd->shd", dscores, q_heads).reshape(queries.shape).astype(jnp.bfloat16)
    return (dquery, dkey, dvalue)


def rows_total_sum(values):
    return lax.psum(values, "rows")


def head_total(values):
    return lax.psum(values.astype(jnp.bfloat16), "tp").astype(jnp.float32)


def regroup(values):
    return lax.all_to_all(values, "rows", split_axis=0, concat_axis=0, tiled=True)


def body(
    features,
    gn_gain,
    conv_w,
    patch_w,
    pos_emb,
    ln1_gain,
    qkv_w,
    out_w,
    final_gain,
    head_w,
    owner_slot,
):
    slab_imgs, rows_here, _, flat_width = features.shape
    col_count = W
    chan_count = flat_width // col_count
    row_devices = lax.axis_size("rows")
    rows_total = rows_here * row_devices
    groups_here = GROUPS * chan_count // C
    group_width = chan_count // groups_here
    count_group = rows_total * col_count * group_width
    own_count = slab_imgs // row_devices
    half_patch = PATCH // 2
    patch_rows = rows_total // half_patch
    patch_cols = col_count // half_patch

    def channel_group_sums(flat):
        per_col = jnp.sum(flat, axis=1).reshape(slab_imgs, col_count, chan_count)
        per_chan = jnp.sum(per_col, axis=1)
        return jnp.sum(per_chan.reshape(slab_imgs, groups_here, group_width), axis=2)

    def spread_flat(per_group):
        return jnp.tile(jnp.repeat(per_group, group_width, axis=1), (1, col_count))[:, None, :]

    feat_float = features.reshape(slab_imgs, rows_here, flat_width).astype(jnp.float32)
    stat_sums = rows_total_sum(
        jnp.stack([channel_group_sums(feat_float), channel_group_sums(feat_float * feat_float)])
    )
    average = stat_sums[0] / count_group
    inverse = lax.rsqrt(stat_sums[1] / count_group - average * average + EPS_GROUP)
    gain_flat = jnp.tile(gn_gain, col_count)[None, None, :]
    normed = (feat_float - spread_flat(average)) * spread_flat(inverse)
    scaled = normed * gain_flat
    active, slope_silu = silu_parts(scaled)
    active = active.astype(jnp.bfloat16)
    kernel_rows = conv_w.reshape(27, chan_count)
    widened = jnp.pad(active, ((0, 0), (2, 2), (0, 0)))
    block_rows = widened.shape[1]
    padded = jnp.pad(widened, ((0, 0), (0, 0), (chan_count, chan_count)))
    terms = lax.dot_general(
        kernel_rows,
        padded.reshape(-1, chan_count),
        (((1,), (1,)), ((), ())),
        preferred_element_type=jnp.float32,
    )
    shifted_terms = terms.reshape(3, 3, 3, slab_imgs, block_rows, col_count + 2)
    out_rows = rows_here + 2
    total = jnp.zeros((3, slab_imgs, out_rows, col_count), jnp.float32)
    for shifted_offset_y in range(3):
        for shifted_offset_x in range(3):
            total = (
                total
                + shifted_terms[
                    :,
                    shifted_offset_y,
                    shifted_offset_x,
                    :,
                    shifted_offset_y : shifted_offset_y + out_rows,
                    shifted_offset_x : shifted_offset_x + col_count,
                ]
            )
    edges = jnp.concatenate([total[:, :, :1], total[:, :, -1:]], axis=2)
    edges_rim = padded_2(edges, (("rows", 2),), 1)
    middle = total[:, :, 1:-1]
    partial_rgb = (
        middle.at[:, :, 0:1].add(edges_rim[:, :, 0:1]).at[:, :, -1:].add(edges_rim[:, :, 3:4])
    )
    picture = head_total(partial_rgb).astype(jnp.bfloat16)
    slot_of = owner_slot[0]
    slot_ids = jnp.arange(slab_imgs, dtype=jnp.int32)
    selector = (slot_of[None, :] == slot_ids[:, None]).astype(jnp.bfloat16)
    by_image = picture.transpose(1, 0, 2, 3).reshape(slab_imgs, -1)
    ordered = jnp.dot(selector, by_image, preferred_element_type=jnp.float32).astype(jnp.bfloat16)
    outgoing = ordered.reshape(row_devices, own_count, 3, rows_here, col_count)
    arrived = regroup(outgoing)
    owned_images = arrived.transpose(1, 2, 0, 3, 4).reshape(own_count, 3, rows_total, col_count)
    gathered = (
        lax.all_gather(qkv_w, "rows", axis=0, tiled=True),
        lax.all_gather(out_w, "rows", axis=0, tiled=True),
        lax.all_gather(patch_w, "rows", axis=0, tiled=True),
    )
    qkv_half = gathered[0]
    out_half = gathered[1]
    patch_full = gathered[2]
    entry_index = jnp.arange(3 * PATCH * PATCH, dtype=jnp.int32)
    colour = entry_index % 3
    pixel_index = entry_index // 3
    target = (
        colour * half_patch * half_patch
        + pixel_index // PATCH // 2 * half_patch
        + pixel_index % PATCH // 2
    )
    fold_table = (
        target[:, None] == jnp.arange(3 * half_patch * half_patch, dtype=jnp.int32)[None, :]
    ).astype(jnp.float32)
    folded_weight = jnp.dot(
        patch_full.astype(jnp.float32), fold_table, precision=lax.Precision.HIGHEST
    )

    def forward_one(picture_one):
        patch_cells = picture_one.reshape(
            3, patch_rows, half_patch, patch_cols, half_patch
        ).transpose(1, 3, 0, 2, 4)
        patch_cells = patch_cells.reshape(
            patch_rows * patch_cols, 3 * half_patch * half_patch
        ).astype(jnp.float32)
        embedded = jnp.dot(
            patch_cells, folded_weight.T, precision=lax.Precision.HIGHEST
        ) + pos_emb.astype(jnp.float32)
        normed_in, hat_in, inv_in = layer_norm(embedded, ln1_gain)
        normed_round = normed_in.astype(jnp.bfloat16)
        queries = jnp.dot(
            normed_round, qkv_half[:, 0, :], preferred_element_type=jnp.float32
        ).astype(jnp.bfloat16)
        key_rows = jnp.dot(
            normed_round, qkv_half[:, 1, :], preferred_element_type=jnp.float32
        ).astype(jnp.bfloat16)
        value_rows = jnp.dot(
            normed_round, qkv_half[:, 2, :], preferred_element_type=jnp.float32
        ).astype(jnp.bfloat16)
        attended = attend(queries, key_rows, value_rows)
        mixed_out = head_total(jnp.dot(attended, out_half.T, preferred_element_type=jnp.float32))
        residual_out = embedded + mixed_out
        pooled = jnp.mean(residual_out, axis=0)
        pooled_out, hat_z, inv_z = layer_norm(pooled, final_gain)
        reward = jnp.sum(pooled_out * head_w)
        return (reward, (hat_in, inv_in, queries, key_rows, value_rows, hat_z, inv_z))

    rewards, stored = lax.map(forward_one, owned_images)

    def backward_one(saved_one):
        hat_in, inv_in, queries, key_rows, value_rows, hat_z, inv_z = saved_one
        upstream = layer_norm_back(head_w, hat_z, inv_z, final_gain)
        row_round = upstream.astype(jnp.bfloat16)[None, :]
        head_grad = jnp.dot(row_round, out_half, preferred_element_type=jnp.float32).astype(
            jnp.bfloat16
        )
        head_grad = jnp.broadcast_to(head_grad, queries.shape)
        dquery, dkey, dvalue = attend_back(queries, key_rows, value_rows, head_grad)
        partial_value = jnp.dot(dquery, qkv_half[:, 0, :].T, preferred_element_type=jnp.float32)
        partial_value = partial_value + jnp.dot(
            dkey, qkv_half[:, 1, :].T, preferred_element_type=jnp.float32
        )
        partial_value = partial_value + jnp.dot(
            dvalue, qkv_half[:, 2, :].T, preferred_element_type=jnp.float32
        )
        dnormed = head_total(partial_value)
        dembedded = upstream[None, :] + layer_norm_back(dnormed, hat_in, inv_in, ln1_gain)
        cell_grads = jnp.dot(round_half(dembedded), folded_weight, precision=lax.Precision.HIGHEST)
        cell_grads = cell_grads.reshape(
            patch_rows, patch_cols, 3, half_patch, half_patch
        ).transpose(2, 0, 3, 1, 4)
        return cell_grads.reshape(3, rows_total, col_count).astype(jnp.bfloat16)

    back_owned = lax.map(backward_one, stored)
    outgoing_back = back_owned.reshape(own_count, 3, row_devices, rows_here, col_count).transpose(
        2, 0, 1, 3, 4
    )
    returned = regroup(outgoing_back)
    by_slot = returned.reshape(slab_imgs, -1)
    dpicture = jnp.dot(selector.T, by_slot, preferred_element_type=jnp.float32).astype(jnp.bfloat16)
    dpicture = dpicture.reshape(slab_imgs, 3, rows_here, col_count).transpose(1, 0, 2, 3)
    grad_rimmed = padded_2(dpicture, (("rows", 2),), 1)
    grad_padded = jnp.pad(grad_rimmed, ((0, 0), (0, 0), (0, 0), (1, 1)))
    windows = []
    for offset_y in range(3):
        for offset_x in range(3):
            windows.append(
                grad_padded[
                    :,
                    :,
                    2 - offset_y : 2 - offset_y + rows_here,
                    2 - offset_x : 2 - offset_x + col_count,
                ]
            )
    stacked = jnp.stack(windows, axis=1).reshape(27, -1)
    dactive = lax.dot_general(
        stacked, kernel_rows, (((0,), (0,)), ((), ())), preferred_element_type=jnp.float32
    )
    dactive = dactive.reshape(slab_imgs, rows_here, flat_width)
    gated_grad = dactive * slope_silu * gain_flat
    back_sums = rows_total_sum(
        jnp.stack([channel_group_sums(gated_grad), channel_group_sums(gated_grad * normed)])
    )
    back_one = back_sums[0] / count_group
    back_two = back_sums[1] / count_group
    grad_features = spread_flat(inverse) * (
        gated_grad - spread_flat(back_one) - normed * spread_flat(back_two)
    )
    grad_out = grad_features.astype(jnp.bfloat16).reshape(slab_imgs, rows_here, 1, flat_width)
    return (grad_out, rewards)


def solution(mesh):
    placed = (
        P(("grp", "img"), "rows", "tp", None),
        P("tp"),
        P(None, None, None, "tp"),
        P("rows", None),
        P(),
        P(),
        P("rows", None, "tp"),
        P("rows", "tp"),
        P(),
        P(),
        P(("grp", "img"), None),
    )
    return jax.shard_map(
        body,
        mesh=mesh,
        in_specs=placed,
        out_specs=(P(("grp", "img"), "rows", "tp", None), P(("grp", "img", "rows"))),
        check_vma=False,
    )
```

profile of v0, /device:TPU:0, one launch (start us, length us, event | category | flops | bytes accessed | tf_op | source)
XLA Modules:
  0.0 287.5 jit_solution(1016339752901137906)
XLA Ops:
  10.3 13.6 %psum.37 = f32[2,4,16]{2,1,0:T(4,128)S(1)} all-reduce(f32[2,4,16]{2,1,0:T(4,128)S(1)} %pad_maximum_fusion.2), channel_id=1, replica_groups=mesh['grp'=2,'rows'=4,'img'=2,'tp'=2] {'rows'}, use_global_device_ids=true, to_apply=%region_6.0 | all-reduce | flops 128 | bytes 1024 | tf_op jit(solution)/shard_map/psum | solution.py:97
  31.0 4.7 %collective-permute-done.1 = f32[3,4,1,112]{3,2,1,0:T(1,128)S(1)} collective-permute-done((f32[3,4,1,112]{3,2,1,0:T(1,128)S(1)}, f32[3,4,1,112]{3,2,1,0:T(1,128)S(1)}, u32[]{:S(2)}, u32[]{:S(2)}) %collective-permute-start.1) | collective-permute-done | bytes 5408 | tf_op jit(solution)/shard_map/ppermute | solution.py:24
  36.0 3.4 %psum.38 = bf16[4,2352]{1,0:T(4,128)(2,1)S(1)} all-reduce(bf16[4,2352]{1,0:T(4,128)(2,1)S(1)} %reshape.369), channel_id=1, replica_groups=mesh['grp'=2,'rows'=4,'img'=2,'tp'=2] {'tp'}, use_global_device_ids=true, to_apply=%region_7.8 | all-reduce | flops 9408 | bytes 37632 | tf_op jit(solution)/shard_map/psum | solution.py:101
  40.2 3.3 %all-to-all-start = ((bf16[4,1,3,7,112]{4,3,2,1,0:T(8,128)(2,1)}), bf16[4,1,3,7,112]{4,3,2,1,0:T(8,128)(2,1)S(1)}, u32[]{:S(2)}, u32[]{:S(2)}) async-start(bf16[4,1,3,7,112]{4,3,2,1,0:T(8,128)(2,1)} %bitcast.9), calls=%async_computation | async-start | bytes 49152 | tf_op jit(solution)/shard_map/all_to_all | solution.py:105
  43.6 5.6 %all-to-all-done = bf16[4,1,3,7,112]{4,3,2,1,0:T(8,128)(2,1)S(1)} async-done(((bf16[4,1,3,7,112]{4,3,2,1,0:T(8,128)(2,1)}), bf16[4,1,3,7,112]{4,3,2,1,0:T(8,128)(2,1)S(1)}, u32[]{:S(2)}, u32[]{:S(2)}) %all-to-all-start) | async-done | bytes 18848 | tf_op jit(solution)/shard_map/all_to_all | solution.py:105
  51.1 2.3 fusion.56
  54.3 89.8 %all-gather.6.cloned.1.call-done = bf16[1280,3,640]{2,0,1:T(8,128)(2,1)} async-done(((bf16[320,3,640]{2,0,1:T(8,128)(2,1)}), bf16[1280,3,640]{2,0,1:T(8,128)(2,1)}) %all-gather.6.cloned.1.call-update) | async-done | bytes 4915216 | tf_op jit(solution)/shard_map/all_gather | solution.py:195
  144.2 1.8 fusion.20
  146.2 1.9 fusion.19
  148.6 1.9 fusion.21
  151.8 30.6 %all-gather.8.cloned.1.call-done = bf16[1280,640]{1,0:T(8,128)(2,1)} async-done(((bf16[320,640]{1,0:T(8,128)(2,1)}), bf16[1280,640]{1,0:T(8,128)(2,1)}) %all-gather.8.cloned.1.call-update) | async-done | bytes 1638416 | tf_op jit(solution)/shard_map/all_gather | solution.py:196
  182.4 2.9 convolution_convert_fusion.2
  185.5 16.8 %all-reduce.6.cloned.1.call-done = bf16[64,1280]{1,0:T(8,128)(2,1)} async-done(((bf16[64,1280]{1,0:T(8,128)(2,1)}), bf16[64,1280]{1,0:T(8,128)(2,1)}) %all-reduce.6.cloned.1.call-update) | async-done | bytes 163856 | tf_op jit(solution)/shard_map/while/body/eval_jaxpr/psum | solution.py:101
  205.8 1.9 multiply_reduce_fusion.3
  214.4 2.0 fusion.4
  216.4 2.0 convolution_add_fusion.1
  218.5 2.7 fusion.2
  221.2 19.3 %all-reduce.8.cloned.1.call-done = bf16[64,1280]{1,0:T(8,128)(2,1)} async-done(((bf16[64,1280]{1,0:T(8,128)(2,1)}), bf16[64,1280]{1,0:T(8,128)(2,1)}) %all-reduce.8.cloned.1.call-update) | async-done | bytes 163856 | tf_op jit(solution)/shard_map/while/body/eval_jaxpr/psum | solution.py:101
  244.7 10.3 %all_to_all.10 = bf16[4,1,3,7,112]{4,3,2,1,0:T(8,128)(2,1)S(1)} all-to-all(bf16[4,1,3,7,112]{4,3,2,1,0:T(8,128)(2,1)S(1)} %copy.63), channel_id=1, replica_groups=mesh['grp'=2,'rows'=4,'img'=2,'tp'=2] {'rows'}, dimensions={0} | all-to-all | bytes 37632 | tf_op jit(solution)/shard_map/all_to_all | solution.py:105
  255.4 2.6 collective-permute-start.2
  259.3 4.2 %collective-permute-done.3 = bf16[3,4,1,112]{3,2,0,1:T(2,128)(2,1)S(1)} collective-permute-done((bf16[3,4,1,112]{3,2,0,1:T(2,128)(2,1)S(1)}, bf16[3,4,1,112]{3,2,0,1:T(2,128)(2,1)S(1)}, u32[]{:S(2)}, u32[]{:S(2)}) %collective-permute-start.3) | collective-permute-done | bytes 2720 | tf_op jit(solution)/shard_map/ppermute | solution.py:24
  264.9 1.4 reshape.380
  266.7 2.2 fusion.122
  269.7 8.9 %psum.41 = f32[2,4,16]{2,1,0:T(4,128)S(1)} all-reduce(f32[2,4,16]{2,1,0:T(4,128)S(1)} %pad_maximum_fusion.3), channel_id=1, replica_groups=mesh['grp'=2,'rows'=4,'img'=2,'tp'=2] {'rows'}, use_global_device_ids=true, to_apply=%region_28.29 | all-reduce | flops 128 | bytes 1024 | tf_op jit(solution)/shard_map/psum | solution.py:97
  (184 shorter events, 34.2 us)
Async XLA Ops:
  7.2 44.0 %all-gather.4.cloned.1.call-start = ((), (), s32[]{:S(2)}) async-start(), calls=%async_computation.2 | async-start | bytes 2048000 | tf_op jit(solution)/shard_map/all_gather | solution.py:197
  7.9 136.3 %all-gather.6.cloned.1.call-start = ((), (), s32[]{:S(2)}) async-start(), calls=%async_computation.3 | async-start | bytes 6144000 | tf_op jit(solution)/shard_map/all_gather | solution.py:195
  8.7 173.7 %all-gather.8.cloned.1.call-start = ((), (), s32[]{:S(2)}) async-start(), calls=%async_computation.4 | async-start | bytes 2048000 | tf_op jit(solution)/shard_map/all_gather | solution.py:196
  9.1 15.4 %copy-start.21 = (f32[64]{0:T(128)S(1)}, f32[64]{0:T(128)}, u32[]{:S(2)}) copy-start(f32[64]{0:T(128)} %param.16) | copy-start | bytes 772
  26.9 12.5 %copy-start.19 = (s32[1,4]{1,0:T(1,128)S(1)}, s32[1,4]{1,0:T(1,128)}, u32[]{:S(2)}) copy-start(s32[1,4]{1,0:T(1,128)} %param.25) | copy-start | bytes 52
  28.3 2.6 collective-permute-start
  29.6 6.1 %collective-permute-start.1 = (f32[3,4,1,112]{3,2,1,0:T(1,128)S(1)}, f32[3,4,1,112]{3,2,1,0:T(1,128)S(1)}, u32[]{:S(2)}, u32[]{:S(2)}) collective-permute-start(f32[3,4,1,112]{3,2,1,0:T(1,128)S(1)} %get-tuple-element.136), channel_id=1, source_target_pairs={{4,0},{8,4},{12,8},{5,1},{9,5},{13,9},{6,2},{10,6},{14,10},{7,3},{... | collective-permute-start | bytes 16136 | tf_op jit(solution)/shard_map/ppermute | solution.py:24
  40.2 9.0 %all-to-all-start = ((bf16[4,1,3,7,112]{4,3,2,1,0:T(8,128)(2,1)}), bf16[4,1,3,7,112]{4,3,2,1,0:T(8,128)(2,1)S(1)}, u32[]{:S(2)}, u32[]{:S(2)}) async-start(bf16[4,1,3,7,112]{4,3,2,1,0:T(8,128)(2,1)} %bitcast.9), calls=%async_computation | async-start | bytes 49152 | tf_op jit(solution)/shard_map/all_to_all | solution.py:105
  43.5 158.8 %all-reduce.6.cloned.1.call-start = ((), (), s32[]{:S(2)}) async-start(), calls=%async_computation.5 | async-start | bytes 327680 | tf_op jit(solution)/shard_map/while/body/eval_jaxpr/psum | solution.py:101
  49.6 3.8 %copy-start.8 = (bf16[64,1280]{1,0:T(8,128)(2,1)S(1)}, bf16[64,1280]{1,0:T(8,128)(2,1)}, u32[]{:S(2)}) copy-start(bf16[64,1280]{1,0:T(8,128)(2,1)} %param.19) | copy-start | bytes 491524
  50.5 3.8 %copy-start.9 = (f32[1280]{0:T(1024)S(1)}, f32[1280]{0:T(1024)}, u32[]{:S(2)}) copy-start(f32[1280]{0:T(1024)} %param.20) | copy-start | bytes 15364
  54.0 94.1 %copy-start.14 = (f32[64]{0:T(128)}, f32[64]{0:T(128)S(1)}, u32[]{:S(2)}) copy-start(f32[64]{0:T(128)S(1)} %broadcast_multiply_fusion.2) | copy-start | bytes 772
  54.2 93.9 %copy-start.16 = (f32[64]{0:T(128)}, f32[64]{0:T(128)S(1)}, u32[]{:S(2)}) copy-start(f32[64]{0:T(128)S(1)} %add_rsqrt_fusion) | copy-start | bytes 772
  182.4 27.9 %copy-start.1 = (bf16[1280,640]{1,0:T(8,128)(2,1)S(1)}, bf16[1280,640]{1,0:T(8,128)(2,1)}, u32[]{:S(2)}) copy-start(bf16[1280,640]{1,0:T(8,128)(2,1)} %all-gather.8.cloned.1.call-done) | copy-start | bytes 4915204
  185.3 55.3 %all-reduce.8.cloned.1.call-start = ((), (), s32[]{:S(2)}) async-start(), calls=%async_computation.6 | async-start | bytes 327680 | tf_op jit(solution)/shard_map/while/body/eval_jaxpr/psum | solution.py:101
  210.6 2.6 copy-start.4
  210.6 2.8 copy-start.6
  218.4 22.1 %copy-start.15 = (f32[64]{0:T(128)S(1)}, f32[64]{0:T(128)}, u32[]{:S(2)}) copy-start(f32[64]{0:T(128)} %copy-done.14) | copy-start | bytes 772
  218.4 22.1 %copy-start.17 = (f32[64]{0:T(128)S(1)}, f32[64]{0:T(128)}, u32[]{:S(2)}) copy-start(f32[64]{0:T(128)} %copy-done.16) | copy-start | bytes 772
  218.5 23.3 %copy-start.12 = (f32[1280]{0:T(1024)S(1)}, f32[1280]{0:T(1024)}, u32[]{:S(2)}) copy-start(f32[1280]{0:T(1024)} %get-tuple-element.134) | copy-start | bytes 15364
  221.2 33.8 %copy-start.20 = (s32[1,4]{1,0:T(1,128)S(1)}, s32[1,4]{1,0:T(1,128)}, u32[]{:S(2)}) copy-start(s32[1,4]{1,0:T(1,128)} %param.25) | copy-start | bytes 52
  242.8 21.6 %copy-start.11 = (bf16[27,64]{1,0:T(8,128)(2,1)S(1)}, bf16[27,64]{1,0:T(8,128)(2,1)}, u32[]{:S(2)}) copy-start(bf16[27,64]{1,0:T(8,128)(2,1)} %copy-done.10) | copy-start | bytes 10372
  255.4 3.9 %collective-permute-start.2 = (bf16[3,4,1,112]{3,2,0,1:T(2,128)(2,1)S(1)}, bf16[3,4,1,112]{3,2,0,1:T(2,128)(2,1)S(1)}, u32[]{:S(2)}, u32[]{:S(2)}) collective-permute-start(bf16[3,4,1,112]{3,2,0,1:T(2,128)(2,1)S(1)} %get-tuple-element.138), channel_id=1, source_target_pairs={{0,4},{4,8},{8,12},{1,5},{5,9},{9,13},{2,6},{6,10},{10,14},{3,7},{... | collective-permute-start | bytes 8072 | tf_op jit(solution)/shard_map/ppermute | solution.py:21
  258.0 5.5 %collective-permute-start.3 = (bf16[3,4,1,112]{3,2,0,1:T(2,128)(2,1)S(1)}, bf16[3,4,1,112]{3,2,0,1:T(2,128)(2,1)S(1)}, u32[]{:S(2)}, u32[]{:S(2)}) collective-permute-start(bf16[3,4,1,112]{3,2,0,1:T(2,128)(2,1)S(1)} %get-tuple-element.139), channel_id=1, source_target_pairs={{4,0},{8,4},{12,8},{5,1},{9,5},{13,9},{6,2},{10,6},{14,10},{7,3},{... | collective-permute-start | bytes 8072 | tf_op jit(solution)/shard_map/ppermute | solution.py:24
  (8 other events, 15.0 us)
Sparse Core Ops, SparseCore 0:
  9.6 41.5 all-gather.3
  52.7 91.4 all-gather.5
  145.7 36.5 all-gather.7
  185.4 16.8 all-reduce.5
  221.3 19.1 all-reduce.7
where the time goes:
time: 288 us
  waiting for transfers between devices  173 us (60%)
  blocking collectives  36.1 us (13%)
  matrix products  22.4 us (8%)
  between operations  17.2 us (6%)
  local copies, waits for them, and re-layouts  14.3 us (5%)
  other arithmetic  14.2 us (5%)
  starting transfers between devices  10.1 us (4%)
    all_gather x1, waiting for transfers between devices, body(): lax.all_gather(qkv_w, 'rows', axis=0, tiled=True)  89.8 us
    psum x2, waiting for transfers between devices, head_total(): return lax.psum(values.astype(jnp.bfloat16), 'tp').astype(jnp.float32)  36.1 us
    all_gather x1, waiting for transfers between devices, body(): lax.all_gather(out_w, 'rows', axis=0, tiled=True)  30.6 us
    psum x2, blocking collectives, rows_total_sum(): return lax.psum(values, 'rows')  22.4 us
    all_to_all x1, blocking collectives, regroup(): lax.all_to_all(values, 'rows', split_axis=0, concat_axis=0, tiled=True)  10.3 us
    ppermute x2, waiting for transfers between devices, padded_2(): lax.ppermute(lax.slice_in_dim(block, 0, width, axis=dim), axis, backward)  8.91 us
  transfers between devices with their start and end apart: 10, of which 8 were waited for; matrix products, arithmetic and copies ran while one was open for 7% of the time, Pallas kernels for 0%

commit v1 on v0

--- a/solution.py
+++ b/solution.py
@@ -98,7 +98,7 @@
 
 
 def head_total(values):
-    return lax.psum(values.astype(jnp.bfloat16), "tp").astype(jnp.float32)
+    return jnp.sum(lax.all_gather(values.astype(jnp.bfloat16), "tp"), axis=0).astype(jnp.float32)
 
 
 def regroup(values):

time: 288 us -> 253 us (0.88)
  waiting for transfers between devices: 173 us -> 139 us
    psum x2 -> x0, waiting for transfers between devices: 36.1 us -> none  [head_total(): return lax.psum(values.astype(jnp.bfloat16), 'tp').astype(jnp.float32)]
    all_gather x0 -> x3, blocking collectives: none -> 6.23 us  [head_total(): lax.all_gather(values.astype(jnp.bfloat16), 'tp')]
    psum x1 -> x0, blocking collectives: 3.41 us -> none  [head_total(): return lax.psum(values.astype(jnp.bfloat16), 'tp').astype(jnp.float32)]
  transfers between devices with their start and end apart: 10 -> 8, of which waited for: 8 -> 6; matrix products, arithmetic and copies ran while one was open for 7% -> 7% of each run, Pallas kernels for 0% -> 0%
where the time goes in v1:
time: 253 us; the launch traced here: 252 us
  waiting for transfers between devices  139 us (55%)
  blocking collectives  36.7 us (15%)
  matrix products  21 us (8%)
  between operations  17.2 us (7%)
  local copies, waits for them, and re-layouts  14.4 us (6%)
  other arithmetic  14.1 us (6%)
  starting transfers between devices  9.85 us (4%)
    all_gather x1, waiting for transfers between devices, body(): lax.all_gather(qkv_w, 'rows', axis=0, tiled=True)  89.8 us
    all_gather x1, waiting for transfers between devices, body(): lax.all_gather(out_w, 'rows', axis=0, tiled=True)  30.6 us
    psum x2, blocking collectives, rows_total_sum(): return lax.psum(values, 'rows')  22.4 us
    ppermute x2, waiting for transfers between devices, padded_2(): lax.ppermute(lax.slice_in_dim(block, 0, width, axis=dim), axis, backward)  8.8 us
    all_to_all x1, blocking collectives, regroup(): lax.all_to_all(values, 'rows', split_axis=0, concat_axis=0, tiled=True)  7.99 us
    all_gather x3, blocking collectives, head_total(): lax.all_gather(values.astype(jnp.bfloat16), 'tp')  6.23 us
    all_to_all x1, waiting for transfers between devices, regroup(): lax.all_to_all(values, 'rows', split_axis=0, concat_axis=0, tiled=True)  6.11 us
  transfers between devices with their start and end apart: 8, of which 6 were waited for; matrix products, arithmetic and copies ran while one was open for 7% of the time, Pallas kernels for 0%

profile of v1, /device:TPU:0, one launch (start us, length us, event | category | flops | bytes accessed | tf_op | source)
XLA Modules:
  0.0 251.9 jit_solution(4043050389631846924)
XLA Ops:
  10.3 13.6 %psum.14 = f32[2,4,16]{2,1,0:T(4,128)S(1)} all-reduce(f32[2,4,16]{2,1,0:T(4,128)S(1)} %pad_maximum_fusion.2), channel_id=1, replica_groups=mesh['grp'=2,'rows'=4,'img'=2,'tp'=2] {'rows'}, use_global_device_ids=true, to_apply=%region_6.0 | all-reduce | flops 128 | bytes 1024 | tf_op jit(solution)/shard_map/psum | solution.py:97
  31.2 4.6 %collective-permute-done.1 = f32[3,4,1,112]{3,1,2,0:T(4,128)S(1)} collective-permute-done((f32[3,4,1,112]{3,1,2,0:T(4,128)S(1)}, f32[3,4,1,112]{3,1,2,0:T(4,128)S(1)}, u32[]{:S(2)}, u32[]{:S(2)}) %collective-permute-start.1) | collective-permute-done | bytes 5408 | tf_op jit(solution)/shard_map/ppermute | solution.py:24
  35.8 1.8 all-gather
  38.6 3.3 %all-to-all-start = ((bf16[4,1,3,7,112]{4,3,2,1,0:T(8,128)(2,1)}), bf16[4,1,3,7,112]{4,3,2,1,0:T(8,128)(2,1)S(1)}, u32[]{:S(2)}, u32[]{:S(2)}) async-start(bf16[4,1,3,7,112]{4,3,2,1,0:T(8,128)(2,1)} %bitcast.10), calls=%async_computation | async-start | bytes 49152 | tf_op jit(solution)/shard_map/all_to_all | solution.py:105
  41.9 6.1 %all-to-all-done = bf16[4,1,3,7,112]{4,3,2,1,0:T(8,128)(2,1)S(1)} async-done(((bf16[4,1,3,7,112]{4,3,2,1,0:T(8,128)(2,1)}), bf16[4,1,3,7,112]{4,3,2,1,0:T(8,128)(2,1)S(1)}, u32[]{:S(2)}, u32[]{:S(2)}) %all-to-all-start) | async-done | bytes 18848 | tf_op jit(solution)/shard_map/all_to_all | solution.py:105
  49.3 1.8 all-gather.7.cloned.1.call-done
  51.1 2.3 fusion.56
  54.3 89.8 %all-gather.9.cloned.1.call-done = bf16[1280,3,640]{2,0,1:T(8,128)(2,1)} async-done(((bf16[320,3,640]{2,0,1:T(8,128)(2,1)}), bf16[1280,3,640]{2,0,1:T(8,128)(2,1)}) %all-gather.9.cloned.1.call-update) | async-done | bytes 4915216 | tf_op jit(solution)/shard_map/all_gather | solution.py:195
  144.2 1.8 fusion.20
  146.2 1.9 fusion.19
  148.6 1.9 fusion.21
  151.8 30.6 %all-gather.11.cloned.1.call-done = bf16[1280,640]{1,0:T(8,128)(2,1)} async-done(((bf16[320,640]{1,0:T(8,128)(2,1)}), bf16[1280,640]{1,0:T(8,128)(2,1)}) %all-gather.11.cloned.1.call-update) | async-done | bytes 1638416 | tf_op jit(solution)/shard_map/all_gather | solution.py:196
  182.4 2.2 convolution_convert_fusion.2
  184.6 2.4 all-gather.1
  192.2 1.9 multiply_reduce_fusion.3
  200.7 2.0 fusion.4
  202.8 2.0 convolution_add_fusion.1
  204.8 2.0 fusion.2
  206.9 2.0 all-gather.2
  211.3 8.0 %all_to_all.10 = bf16[4,1,3,7,112]{4,3,2,1,0:T(8,128)(2,1)S(1)} all-to-all(bf16[4,1,3,7,112]{4,3,2,1,0:T(8,128)(2,1)S(1)} %copy.98), channel_id=1, replica_groups=mesh['grp'=2,'rows'=4,'img'=2,'tp'=2] {'rows'}, dimensions={0} | all-to-all | bytes 37632 | tf_op jit(solution)/shard_map/all_to_all | solution.py:105
  219.7 2.6 %collective-permute-start.2 = (bf16[3,4,1,112]{3,2,0,1:T(2,128)(2,1)S(1)}, bf16[3,4,1,112]{3,2,0,1:T(2,128)(2,1)S(1)}, u32[]{:S(2)}, u32[]{:S(2)}) collective-permute-start(bf16[3,4,1,112]{3,2,0,1:T(2,128)(2,1)S(1)} %get-tuple-element.149), channel_id=1, source_target_pairs={{0,4},{4,8},{8,12},{1,5},{5,9},{9,13},{2,6},{6,10},{10,14},{3,7},{... | collective-permute-start | bytes 8072 | tf_op jit(solution)/shard_map/ppermute | solution.py:21
  223.7 4.2 %collective-permute-done.3 = bf16[3,4,1,112]{3,2,0,1:T(2,128)(2,1)S(1)} collective-permute-done((bf16[3,4,1,112]{3,2,0,1:T(2,128)(2,1)S(1)}, bf16[3,4,1,112]{3,2,0,1:T(2,128)(2,1)S(1)}, u32[]{:S(2)}, u32[]{:S(2)}) %collective-permute-start.3) | collective-permute-done | bytes 2720 | tf_op jit(solution)/shard_map/ppermute | solution.py:24
  231.1 2.2 fusion.124
  234.1 8.9 %psum.15 = f32[2,4,16]{2,1,0:T(4,128)S(1)} all-reduce(f32[2,4,16]{2,1,0:T(4,128)S(1)} %pad_maximum_fusion.3), channel_id=1, replica_groups=mesh['grp'=2,'rows'=4,'img'=2,'tp'=2] {'rows'}, use_global_device_ids=true, to_apply=%region_28.29 | all-reduce | flops 128 | bytes 1024 | tf_op jit(solution)/shard_map/psum | solution.py:97
  (182 shorter events, 34.7 us)
Async XLA Ops:
  7.2 44.0 %all-gather.7.cloned.1.call-start = ((), (), s32[]{:S(2)}) async-start(), calls=%async_computation.2 | async-start | bytes 2048000 | tf_op jit(solution)/shard_map/all_gather | solution.py:197
  7.9 136.3 %all-gather.9.cloned.1.call-start = ((), (), s32[]{:S(2)}) async-start(), calls=%async_computation.3 | async-start | bytes 6144000 | tf_op jit(solution)/shard_map/all_gather | solution.py:195
  8.7 173.7 %all-gather.11.cloned.1.call-start = ((), (), s32[]{:S(2)}) async-start(), calls=%async_computation.4 | async-start | bytes 2048000 | tf_op jit(solution)/shard_map/all_gather | solution.py:196
  9.1 15.4 %copy-start.21 = (f32[64]{0:T(128)S(1)}, f32[64]{0:T(128)}, u32[]{:S(2)}) copy-start(f32[64]{0:T(128)} %param.16) | copy-start | bytes 772
  28.1 9.7 %copy-start.19 = (s32[1,4]{1,0:T(1,128)S(1)}, s32[1,4]{1,0:T(1,128)}, u32[]{:S(2)}) copy-start(s32[1,4]{1,0:T(1,128)} %param.25) | copy-start | bytes 52
  28.5 2.6 %collective-permute-start = (f32[3,4,1,112]{3,1,2,0:T(4,128)S(1)}, f32[3,4,1,112]{3,1,2,0:T(4,128)S(1)}, u32[]{:S(2)}, u32[]{:S(2)}) collective-permute-start(f32[3,4,1,112]{3,1,2,0:T(4,128)S(1)} %get-tuple-element.148), channel_id=1, source_target_pairs={{0,4},{4,8},{8,12},{1,5},{5,9},{9,13},{2,6},{6,10},{10,14},{3,7},{... | collective-permute-start | bytes 16136 | tf_op jit(solution)/shard_map/ppermute | solution.py:21
  29.8 6.0 %collective-permute-start.1 = (f32[3,4,1,112]{3,1,2,0:T(4,128)S(1)}, f32[3,4,1,112]{3,1,2,0:T(4,128)S(1)}, u32[]{:S(2)}, u32[]{:S(2)}) collective-permute-start(f32[3,4,1,112]{3,1,2,0:T(4,128)S(1)} %get-tuple-element.147), channel_id=1, source_target_pairs={{4,0},{8,4},{12,8},{5,1},{9,5},{13,9},{6,2},{10,6},{14,10},{7,3},{... | collective-permute-start | bytes 16136 | tf_op jit(solution)/shard_map/ppermute | solution.py:24
  38.6 9.4 %all-to-all-start = ((bf16[4,1,3,7,112]{4,3,2,1,0:T(8,128)(2,1)}), bf16[4,1,3,7,112]{4,3,2,1,0:T(8,128)(2,1)S(1)}, u32[]{:S(2)}, u32[]{:S(2)}) async-start(bf16[4,1,3,7,112]{4,3,2,1,0:T(8,128)(2,1)} %bitcast.10), calls=%async_computation | async-start | bytes 49152 | tf_op jit(solution)/shard_map/all_to_all | solution.py:105
  48.5 4.9 %copy-start.8 = (bf16[64,1280]{1,0:T(8,128)(2,1)S(1)}, bf16[64,1280]{1,0:T(8,128)(2,1)}, u32[]{:S(2)}) copy-start(bf16[64,1280]{1,0:T(8,128)(2,1)} %param.19) | copy-start | bytes 491524
  49.3 4.9 %copy-start.9 = (f32[1280]{0:T(1024)S(1)}, f32[1280]{0:T(1024)}, u32[]{:S(2)}) copy-start(f32[1280]{0:T(1024)} %param.20) | copy-start | bytes 15364
  54.0 94.1 %copy-start.14 = (f32[64]{0:T(128)}, f32[64]{0:T(128)S(1)}, u32[]{:S(2)}) copy-start(f32[64]{0:T(128)S(1)} %broadcast_multiply_fusion.2) | copy-start | bytes 772
  54.2 93.9 %copy-start.16 = (f32[64]{0:T(128)}, f32[64]{0:T(128)S(1)}, u32[]{:S(2)}) copy-start(f32[64]{0:T(128)S(1)} %add_rsqrt_fusion) | copy-start | bytes 772
  146.2 2.4 copy-start.3
  148.5 2.5 copy-start.18
  182.4 14.3 %copy-start.1 = (bf16[1280,640]{1,0:T(8,128)(2,1)S(1)}, bf16[1280,640]{1,0:T(8,128)(2,1)}, u32[]{:S(2)}) copy-start(bf16[1280,640]{1,0:T(8,128)(2,1)} %all-gather.11.cloned.1.call-done) | copy-start | bytes 4915204
  197.0 2.6 %copy-start.4 = (bf16[64,8,80]{2,1,0:T(8,128)(2,1)S(1)}, bf16[64,8,80]{2,1,0:T(8,128)(2,1)}, u32[]{:S(2)}) copy-start(bf16[64,8,80]{2,1,0:T(8,128)(2,1)} %copy-done.3) | copy-start | bytes 245764
  197.0 2.8 %copy-start.6 = (bf16[64,8,80]{2,1,0:T(8,128)(2,1)S(1)}, bf16[64,8,80]{2,1,0:T(8,128)(2,1)}, u32[]{:S(2)}) copy-start(bf16[64,8,80]{2,1,0:T(8,128)(2,1)} %copy-done.5) | copy-start | bytes 245764
  204.8 4.2 %copy-start.15 = (f32[64]{0:T(128)S(1)}, f32[64]{0:T(128)}, u32[]{:S(2)}) copy-start(f32[64]{0:T(128)} %copy-done.14) | copy-start | bytes 772
  204.8 4.2 %copy-start.17 = (f32[64]{0:T(128)S(1)}, f32[64]{0:T(128)}, u32[]{:S(2)}) copy-start(f32[64]{0:T(128)} %copy-done.16) | copy-start | bytes 772
  204.8 4.4 %copy-start.12 = (f32[1280]{0:T(1024)S(1)}, f32[1280]{0:T(1024)}, u32[]{:S(2)}) copy-start(f32[1280]{0:T(1024)} %get-tuple-element.136) | copy-start | bytes 15364
  209.0 10.4 %copy-start.20 = (s32[1,4]{1,0:T(1,128)S(1)}, s32[1,4]{1,0:T(1,128)}, u32[]{:S(2)}) copy-start(s32[1,4]{1,0:T(1,128)} %param.25) | copy-start | bytes 52
  209.5 19.3 %copy-start.11 = (bf16[27,64]{1,0:T(8,128)(2,1)S(1)}, bf16[27,64]{1,0:T(8,128)(2,1)}, u32[]{:S(2)}) copy-start(bf16[27,64]{1,0:T(8,128)(2,1)} %copy-done.10) | copy-start | bytes 10372
  219.7 3.9 %collective-permute-start.2 = (bf16[3,4,1,112]{3,2,0,1:T(2,128)(2,1)S(1)}, bf16[3,4,1,112]{3,2,0,1:T(2,128)(2,1)S(1)}, u32[]{:S(2)}, u32[]{:S(2)}) collective-permute-start(bf16[3,4,1,112]{3,2,0,1:T(2,128)(2,1)S(1)} %get-tuple-element.149), channel_id=1, source_target_pairs={{0,4},{4,8},{8,12},{1,5},{5,9},{9,13},{2,6},{6,10},{10,14},{3,7},{... | collective-permute-start | bytes 8072 | tf_op jit(solution)/shard_map/ppermute | solution.py:21
  222.3 5.5 %collective-permute-start.3 = (bf16[3,4,1,112]{3,2,0,1:T(2,128)(2,1)S(1)}, bf16[3,4,1,112]{3,2,0,1:T(2,128)(2,1)S(1)}, u32[]{:S(2)}, u32[]{:S(2)}) collective-permute-start(bf16[3,4,1,112]{3,2,0,1:T(2,128)(2,1)S(1)} %get-tuple-element.150), channel_id=1, source_target_pairs={{4,0},{8,4},{12,8},{5,1},{9,5},{13,9},{6,2},{10,6},{14,10},{7,3},{... | collective-permute-start | bytes 8072 | tf_op jit(solution)/shard_map/ppermute | solution.py:24
  (6 other events, 10.1 us)
Sparse Core Ops, SparseCore 0:
  9.6 41.5 all-gather.6
  52.7 91.4 all-gather.8
  145.7 36.5 all-gather.10
